TPU v7x, 512 devices: a whole 4x8x8 slice. The times are simulated.
512 devices in a mesh: dp: 32 (over y, z_hi, core), space: 16 (over x, z_lo).
Axes of the slice: x: 4, y: 8, z: 8 (z_hi: 2, z_lo: 4; z = z_hi * 4 + z_lo), core: 2. Of those that a mesh axis runs over, the one named last changes fastest.
Arguments:
- scenes: bfloat16 [64, 224, 8, 768], P('dp', 'space'), may hold values from -8 to 8
- kernel: bfloat16 [7, 7, 768], replicated, may hold values from -0.875 to 0.875
- weight_in: bfloat16 [768, 1536], replicated, may hold values from -0.21875 to 0.21875
- weight_out: bfloat16 [1536, 768], replicated, may hold values from -0.15625 to 0.15625
- captions: bfloat16 [64, 768], P('dp'), may hold values from -0.21972656 to 0.21972656
- positives: int32 [64], P('dp'), may hold values from 0 to 63, each once
Outputs:
- loss: float32 [], replicated
- text_grad: float32 [64, 768], P('dp')
- kernel_grad: float32 [7, 7, 768], replicated
Inputs may be any that keep to these rules, and one draw needn't show every extreme that they name: `positives`: every caption index appears exactly once.
All inputs are finite; a program needn't handle non-finite values.
Results may differ from a plain program's by a relative error of at most 0.0054.
Values may be sent and summed in bfloat16 or wider, within the bound.
A program may use at most 64 MiB of HBM per device.

v0:
```python
import jax
import jax.numpy as jnp
from jax import lax
from jax.sharding import PartitionSpec as P

EPS = 1e-06
LOGIT_SCALE = 10.0
LOGIT_BIAS = -1.0
GELU_C = 0.7978845608028654


def with_halo(array, sides, width):
    for axis, dim in sides:
        count, length = (lax.axis_size(axis), array.shape[dim])
        up = [(i, (i + 1) % count) for i in range(count - 1)]
        down = [(j, i) for i, j in up]
        last = lax.slice_in_dim(array, length - width, length, axis=dim)
        first = lax.slice_in_dim(array, 0, width, axis=dim)
        before = lax.ppermute(last, axis, up)
        after = lax.ppermute(first, axis, down)
        array = jnp.concatenate([before, array, after], axis=dim)
    return array


def gelu_tanh(values):
    return 0.5 * values * (1.0 + jnp.tanh(GELU_C * (values + 0.044715 * values * values * values)))


def gelu_slope(values):
    tangent = jnp.tanh(GELU_C * (values + 0.044715 * values * values * values))
    return 0.5 * (1.0 + tangent) + 0.5 * values * (1.0 - tangent * tangent) * GELU_C * (
        1.0 + 3.0 * 0.044715 * values * values
    )


def depthwise(padded, kernel, tile_rows, tile_cols):
    total = jnp.zeros(padded.shape[:-3] + (tile_rows, tile_cols, padded.shape[-1]), jnp.float32)
    for row_shift in range(7):
        for col_shift in range(7):
            total = (
                total
                + kernel[row_shift, col_shift].astype(jnp.float32)
                * padded[
                    ..., row_shift : row_shift + tile_rows, col_shift : col_shift + tile_cols, :
                ]
            )
    return total


def kernel_terms(padded, conv_grad, tile_rows, tile_cols):
    summed_axes = tuple(range(conv_grad.ndim - 1))
    listed = []
    for row_shift in range(7):
        for col_shift in range(7):
            window = padded[
                ..., row_shift : row_shift + tile_rows, col_shift : col_shift + tile_cols, :
            ]
            listed.append(jnp.sum(window * conv_grad, axis=summed_axes))
    return jnp.stack(listed).reshape(7, 7, conv_grad.shape[-1])


def normalize_rows(conv_out):
    center = conv_out - jnp.mean(conv_out, axis=-1, keepdims=True)
    inv_scale = lax.rsqrt(jnp.mean(center * center, axis=-1, keepdims=True) + EPS)
    return (center * inv_scale, inv_scale)


def unit_rows(values):
    norms = jnp.sqrt(jnp.sum(values * values, axis=-1, keepdims=True) + EPS)
    return (values / norms, norms)


def pair_weights(labels, logits):
    return (-labels * jax.nn.sigmoid(-labels * logits)).astype(jnp.bfloat16)


def per_device(scenes, kernel, weight_in, weight_out, captions, positives):
    images, tile_rows, tile_cols, channels = scenes.shape
    hidden_units = weight_in.shape[1]
    space_count = lax.axis_size("space")
    pixels = tile_rows * space_count * tile_cols
    row_padded = with_halo(scenes, (("space", 1),), 3)
    padded = jnp.pad(row_padded.astype(jnp.float32), ((0, 0), (0, 0), (3, 3), (0, 0)))
    conv_out = depthwise(padded, kernel, tile_rows, tile_cols)
    normed, inv_scale = normalize_rows(conv_out)
    flat_rows = normed.reshape(-1, channels).astype(jnp.bfloat16)
    hidden = jnp.dot(flat_rows, weight_in, preferred_element_type=jnp.float32)
    activated = gelu_tanh(hidden).astype(jnp.bfloat16)
    mixed_out = jnp.dot(activated, weight_out, preferred_element_type=jnp.float32)
    block_out = scenes.reshape(-1, channels).astype(jnp.float32) + mixed_out
    tile_sums = jnp.sum(block_out.reshape(images, -1, channels), axis=1)
    pooled = lax.psum(tile_sums, "space") / pixels
    image_unit, pooled_norm = unit_rows(pooled)
    text_unit, text_norm = unit_rows(captions.astype(jnp.float32))
    image_cast = image_unit.astype(jnp.bfloat16)
    gathered = lax.all_gather(captions, "dp", axis=0, tiled=True)
    all_unit, all_norm = unit_rows(gathered.astype(jnp.float32))
    all_cast = all_unit.astype(jnp.bfloat16)
    total_rows = gathered.shape[0]
    logits = (
        LOGIT_SCALE * jnp.dot(image_cast, all_cast.T, preferred_element_type=jnp.float32)
        + LOGIT_BIAS
    )
    labels = jnp.where(
        positives[:, None] == jnp.arange(total_rows, dtype=jnp.int32)[None, :], 1.0, -1.0
    ).astype(jnp.float32)
    loss_part = jnp.sum(jax.nn.softplus(-labels * logits))
    pair_grad = pair_weights(labels, logits)
    image_side = LOGIT_SCALE * jnp.dot(pair_grad, all_cast, preferred_element_type=jnp.float32)
    caption_side = lax.psum_scatter(
        LOGIT_SCALE * jnp.dot(pair_grad.T, image_cast, preferred_element_type=jnp.float32),
        "dp",
        scatter_dimension=0,
        tiled=True,
    )
    text_grad = (
        caption_side - text_unit * jnp.sum(text_unit * caption_side, axis=-1, keepdims=True)
    ) / text_norm
    pooled_grad = (
        image_side - image_unit * jnp.sum(image_unit * image_side, axis=-1, keepdims=True)
    ) / pooled_norm
    slope = (pooled_grad / pixels).astype(jnp.bfloat16)
    act_grad = jnp.dot(slope, weight_out.T, preferred_element_type=jnp.float32)
    hidden_grad = (
        act_grad[:, None, :] * gelu_slope(hidden.reshape(images, -1, hidden_units))
    ).astype(jnp.bfloat16)
    normed_grad = jnp.dot(
        hidden_grad.reshape(-1, hidden_units), weight_in.T, preferred_element_type=jnp.float32
    )
    normed_grad = normed_grad.reshape(images, tile_rows, tile_cols, channels)
    conv_grad = inv_scale * (
        normed_grad
        - jnp.mean(normed_grad, axis=-1, keepdims=True)
        - normed * jnp.mean(normed_grad * normed, axis=-1, keepdims=True)
    )
    kernel_part = kernel_terms(padded, conv_grad, tile_rows, tile_cols)
    loss_share = jnp.where(lax.axis_index("space") == 0, loss_part, jnp.zeros((), jnp.float32))
    kernel_grad, loss_total = lax.psum((kernel_part, loss_share), ("dp", "space"))
    loss = loss_total / (images * lax.axis_size("dp"))
    return (loss, text_grad, kernel_grad)


def solution(mesh):
    return jax.shard_map(
        per_device,
        mesh=mesh,
        in_specs=(P("dp", "space", None, None), P(), P(), P(), P("dp", None), P("dp")),
        out_specs=(P(), P("dp", None), P()),
        check_vma=False,
    )
```

profile of v0, /device:TPU:1, one launch (start us, length us, event | category | flops | bytes accessed | tf_op | source)
XLA Modules:
  0.0 752.9 jit_solution(10114848180464947701)
XLA Ops:
  7.2 0.0 copy-start
  7.2 0.0 all-reduce.7.cloned.1.call-start
  7.2 1.1 fusion.35
  8.3 4.8 collective-permute-start
  13.2 1.3 collective-permute-start.1
  14.5 1.9 convert_reduce_fusion.48
  16.4 2.0 convert_reduce_fusion.47
  18.4 0.8 fusion.16
  19.2 58.3 %all-gather = bf16[32,2,768]{2,1,0:T(2,128)(2,1)S(1)} all-gather(bf16[1,2,768]{2,1,0:T(2,128)(2,1)} %bitcast.27), channel_id=1, replica_groups=mesh['dp'=32,'space'=16] {'dp'}, dimensions={0}, use_global_device_ids=true | all-gather | bytes 101376 | tf_op jit(solution)/shard_map/all_gather | solution.py:96
  77.5 0.1 multiply_reduce_fusion.51
  77.7 0.1 divide_convert_fusion
  77.8 0.6 add_sqrt_fusion
  78.4 1.3 dynamic-slice
  80.3 1.0 convert_reduce_fusion.46
  81.3 1.1 maximum_convert_fusion
  82.4 6.5 fusion.34
  88.9 0.2 multiply_reduce_fusion.50
  89.2 0.1 fusion.15
  89.3 0.0 copy-start.6
  89.3 0.0 copy-start.7
  89.3 0.7 fusion.36
  90.1 0.9 copy-done.6
  91.0 0.2 copy-done.7
  91.1 1.8 convolution_add_fusion
  92.9 1.2 reduce_sum.542
  94.1 38.7 %psum.21 = f32[2,768]{1,0:T(2,128)S(1)} all-reduce(f32[2,768]{1,0:T(2,128)S(1)} %reduce_sum.542), channel_id=1, replica_groups=mesh['dp'=32,'space'=16] {'space'}, use_global_device_ids=true, to_apply=%region_3.4 | all-reduce | flops 1536 | bytes 12288 | tf_op jit(solution)/shard_map/psum | solution.py:92
  132.8 0.1 multiply_reduce_fusion.54
  132.9 0.8 fusion.24
  133.7 0.3 multiply_reduce_fusion.52
  134.0 1.0 convolution_multiply_fusion
  135.0 2.5 fusion.17
  137.6 0.9 fusion.8
  138.5 1.0 fusion.33
  139.5 2.0 multiply_reduce_fusion
  141.5 0.8 copy-done.5
  142.3 1.6 multiply_reduce_fusion.18
  144.8 0.0 all-reduce.7.cloned.1.call-update
  144.9 0.0 all-reduce.5.cloned.1.call-start
  144.9 101.0 %psum.22 = f32[]{:T(128)} all-reduce(f32[]{:T(128)S(6)} %select_n.14), channel_id=1, replica_groups=mesh['dp'=32,'space'=16] {'dp','space'}, use_global_device_ids=true, to_apply=%region_7.8 | all-reduce | flops 1 | bytes 8 | tf_op jit(solution)/shard_map/psum | solution.py:138
  245.9 2.2 multiply_reduce_fusion.36
  248.5 0.3 stack.199
  248.8 0.7 reshape.408
  249.5 0.0 all-reduce.5.cloned.1.call-update
  250.2 223.1 %all-reduce.7.cloned.1.call-done = f32[64,768]{1,0:T(8,128)} async-done(((f32[64,768]{1,0:T(8,128)}), f32[64,768]{1,0:T(8,128)}) %all-reduce.7.cloned.1.call-update) | async-done | bytes 196624
  473.3 0.9 multiply_reduce_fusion.53
  474.2 1.4 subtract_divide_fusion
  475.6 267.8 %all-reduce.5.cloned.1.call-done = f32[7,7,768]{2,1,0:T(8,128)} async-done(((f32[7,7,768]{2,1,0:T(8,128)}), f32[7,7,768]{2,1,0:T(8,128)}) %all-reduce.5.cloned.1.call-update) | async-done | bytes 150544 | tf_op jit(solution)/shard_map/psum | solution.py:138
  743.4 1.6 copy.12
  (73 shorter events, 0.3 us)
Async XLA Ops:
  7.2 82.1 %copy-start = (bf16[768,1536]{1,0:T(8,128)(2,1)S(1)}, bf16[768,1536]{1,0:T(8,128)(2,1)}, u32[]{:S(2)}) copy-start(bf16[768,1536]{1,0:T(8,128)(2,1)} %param.8) | copy-start | bytes 7077892
  7.2 466.1 %all-reduce.7.cloned.1.call-start = ((), (), s32[]{:S(2)}) async-start(), calls=%async_computation.1 | async-start | bytes 393216
  8.3 73.0 %collective-permute-start = (bf16[2,3,8,768]{3,2,1,0:T(8,128)(2,1)S(1)}, bf16[2,3,8,768]{3,2,1,0:T(8,128)(2,1)S(1)}, u32[]{:S(2)}, u32[]{:S(2)}) collective-permute-start(bf16[2,3,8,768]{3,2,1,0:T(8,128)(2,1)S(1)} %get-tuple-element.108), channel_id=1, source_target_pairs={{0,1},{1,2},{2,3},{3,4},{4,5},{5,6},{6,7},{7,8},{8,9},{9,10},{10,1... | collective-permute-start | bytes 221192 | tf_op jit(solution)/shard_map/ppermute | solution.py:19
  13.2 68.1 %collective-permute-start.1 = (bf16[2,3,8,768]{3,2,1,0:T(8,128)(2,1)S(1)}, bf16[2,3,8,768]{3,2,1,0:T(8,128)(2,1)}, u32[]{:S(2)}, u32[]{:S(2)}) collective-permute-start(bf16[2,3,8,768]{3,2,1,0:T(8,128)(2,1)S(1)} %get-tuple-element.109), channel_id=1, source_target_pairs={{1,0},{2,1},{3,2},{4,3},{5,4},{6,5},{7,6},{8,7},{9,8},{10,9},{11,1... | collective-permute-start | bytes 221192 | tf_op jit(solution)/shard_map/ppermute | solution.py:20
  88.9 1.1 copy-start.1
  89.3 1.7 copy-start.6
  89.3 1.8 copy-start.7
  90.0 2.9 copy-start.3
  91.1 41.8 %copy-start.10 = (s32[2]{0:T(128)S(1)}, s32[2]{0:T(128)}, u32[]{:S(2)}) copy-start(s32[2]{0:T(128)} %param.11) | copy-start | bytes 28
  135.0 2.5 copy-start.4
  135.0 3.4 copy-start.2
  141.5 0.9 copy-start.5
  144.9 598.5 %all-reduce.5.cloned.1.call-start = ((), (), s32[]{:S(2)}) async-start(), calls=%async_computation | async-start | bytes 344064 | tf_op jit(solution)/shard_map/psum | solution.py:138
  245.9 227.3 %copy-start.8 = (bf16[2,768]{1,0:T(2,128)(2,1)S(1)}, bf16[2,768]{1,0:T(2,128)(2,1)}, u32[]{:S(2)}) copy-start(bf16[2,768]{1,0:T(2,128)(2,1)} %param.10) | copy-start | bytes 9220
  245.9 227.3 %copy-start.9 = (f32[2]{0:T(128)S(1)}, f32[2]{0:T(128)}, u32[]{:S(2)}) copy-start(f32[2]{0:T(128)} %add_sqrt_fusion) | copy-start | bytes 28
Sparse Core Ops, SparseCore 0:
  145.0 328.2 all-reduce.6
  479.6 263.7 all-reduce.4
where the time goes:
time: 754 us; the launch traced here: 753 us
  waiting for transfers between devices  491 us (65%)
  blocking collectives  198 us (26%)
  other arithmetic  24.8 us (3%)
  between operations  17.7 us (2%)
  matrix products  8.13 us (1%)
    psum x1, waiting for transfers between devices, per_device(): lax.psum((kernel_part, loss_share), ('dp', 'space'))  268 us
    unnamed x3, waiting for transfers between devices  223 us
    psum x1, blocking collectives, per_device(): lax.psum((kernel_part, loss_share), ('dp', 'space'))  101 us
    all_gather x1, blocking collectives, per_device(): gathered = lax.all_gather(captions, 'dp', axis=0, tiled=True)  58.3 us
    psum x1, blocking collectives, per_device(): pooled = lax.psum(tile_sums, 'space') / pixels  38.7 us
  transfers between devices with their start and end apart: 4, of which 2 were waited for; matrix products, arithmetic and copies ran while one was open for 2% of the time, Pallas kernels for 0%

commit v1 on v0

v1 whole, which is shorter than its diff:
```python
import functools

import jax
import jax.numpy as jnp
from jax import lax
from jax.experimental import pallas as pl
from jax.experimental.pallas import tpu as pltpu
from jax.sharding import PartitionSpec as P

EPS = 1e-06
LOGIT_SCALE = 10.0
LOGIT_BIAS = -1.0
GELU_C = 0.7978845608028654
MESH = pl.DeviceIdType.MESH
F32 = jnp.float32
BF16 = jnp.bfloat16
TAPS = 7
HALF = 3
LANES = 128
HID_BLOCK = 256
ROW_BLOCK = 32


def dot_nt(a, b):
    return lax.dot_general(a, b, (((1,), (1,)), ((), ())), preferred_element_type=F32)


def dot_nn(a, b):
    return lax.dot_general(a, b, (((1,), (0,)), ((), ())), preferred_element_type=F32)


def shift_cols(values, offset):
    if offset == 0:
        return values
    cols = values.shape[1]
    col = lax.broadcasted_iota(jnp.int32, values.shape, 1) + offset
    rolled = pltpu.roll(values, (-offset) % cols, axis=1)
    return jnp.where((col >= 0) & (col < cols), rolled, 0.0)


def wait_bytes(ref, sem):
    pltpu.make_async_copy(ref, ref, sem).wait()


def kernel(
    cfg,
    scenes_ref, kernel_ref, w_in_hbm, w_out_hbm, captions_ref, positives_ref,
    loss_ref, text_grad_ref, kernel_grad_ref,
    xf, kf, halo, co, nb, inv, w_in, w_out, gp, asum, ssum, hg, cg, agrad,
    pool, capbuf, cap64, text64, imgbuf, img64, pos64,
    ksend, krecv, kown, p1, p2, kfull,
    wsem, halo_s, halo_r, sib_s, sib_r, cap_s, cap_r, pool_s, pool_r, img_s, img_r,
    p1_s, p1_r, p2_s, p2_r, p3_s, p3_r,
):
    n_space, n_dp = cfg
    n_grp = n_dp // 2
    images, rows, cols, chan = scenes_ref.shape
    hid = w_in_hbm.shape[1]
    tile_pix = rows * cols
    pixels = rows * n_space * cols
    n_img = images * n_dp
    ctiles = chan // LANES
    half_tiles = ctiles // 2
    chunk = p1.shape[1]
    used = half_tiles * TAPS * TAPS

    dp = lax.axis_index("dp")
    sp = lax.axis_index("space")
    core = lax.rem(dp, 2)
    other = 1 - core
    grp = lax.div(dp, 2)
    sib = 2 * grp + other
    first = sp == 0
    last = sp == n_space - 1

    def space_peer(d):
        return lax.rem(sp + d, n_space)

    def grp_peer(d):
        return lax.rem(grp + d, n_grp)

    barrier = pltpu.get_barrier_semaphore()
    pl.semaphore_signal(barrier, inc=1, device_id=(sib, sp), device_id_type=MESH)

    def greet_space(d, _):
        pl.semaphore_signal(barrier, inc=1, device_id=(dp, space_peer(d)), device_id_type=MESH)
        return 0

    def greet_grp(d, _):
        pl.semaphore_signal(
            barrier, inc=1, device_id=(2 * grp_peer(d) + core, sp), device_id_type=MESH
        )
        return 0

    lax.fori_loop(1, n_space, greet_space, 0)
    lax.fori_loop(1, n_grp, greet_grp, 0)

    load_in = pltpu.make_async_copy(w_in_hbm, w_in, wsem.at[0])
    load_out = pltpu.make_async_copy(w_out_hbm, w_out, wsem.at[1])
    load_in.start()
    load_out.start()

    kf[...] = kernel_ref[...].astype(F32)
    capbuf[grp, core] = captions_ref[...]

    def conv_tile(ct, _):
        lanes = pl.ds(pl.multiple_of(ct * LANES, LANES), LANES)
        empty = jnp.zeros((HALF, cols, LANES), F32)
        for img in range(images):
            own = scenes_ref[img, :, :, lanes].astype(F32)
            xf[img, HALF : HALF + rows, :, lanes] = own
            ssum[img : img + 1, lanes] = jnp.sum(
                jnp.sum(own, axis=0), axis=0, keepdims=True
            )
            x = jnp.concatenate([empty, own, empty], axis=0)
            total = jnp.zeros((rows, cols, LANES), F32)
            for j in range(TAPS):
                part = jnp.zeros((rows, cols, LANES), F32)
                for i in range(TAPS):
                    part = part + kf[i, j : j + 1, lanes][None] * x[i : i + rows]
                total = total + shift_cols(part, j - HALF)
            co[img * tile_pix : (img + 1) * tile_pix, lanes] = total.reshape(tile_pix, LANES)
        return 0

    lax.fori_loop(0, ctiles, conv_tile, 0)

    pl.semaphore_wait(barrier, n_space + n_grp - 1)

    def halo_copy(src_row, slot, peer):
        return pltpu.make_async_remote_copy(
            src_ref=scenes_ref.at[:, pl.ds(src_row, HALF)],
            dst_ref=halo.at[slot],
            send_sem=halo_s.at[slot],
            recv_sem=halo_r.at[slot],
            device_id=(dp, peer),
            device_id_type=MESH,
        )

    @pl.when(jnp.logical_not(last))
    def _():
        halo_copy(rows - HALF, 0, sp + 1).start()

    @pl.when(jnp.logical_not(first))
    def _():
        halo_copy(0, 1, sp - 1).start()

    @pl.when(first)
    def _():
        halo[0] = jnp.zeros_like(halo[0])

    @pl.when(last)
    def _():
        halo[1] = jnp.zeros_like(halo[1])

    def sib_copy(src, dst, k):
        return pltpu.make_async_remote_copy(
            src_ref=src, dst_ref=dst, send_sem=sib_s.at[k], recv_sem=sib_r.at[k],
            device_id=(sib, sp), device_id_type=MESH,
        )

    def grp_send(ref, send_sem, recv_sem):
        def step(d, _):
            pltpu.make_async_remote_copy(
                src_ref=ref, dst_ref=ref, send_sem=send_sem, recv_sem=recv_sem,
                device_id=(2 * grp_peer(d) + core, sp), device_id_type=MESH,
            ).start()
            return 0

        lax.fori_loop(1, n_grp, step, 0)

    def space_send(ref_of, dst, send_sem, recv_sem):
        def step(d, _):
            peer = space_peer(d)
            pltpu.make_async_remote_copy(
                src_ref=ref_of(peer), dst_ref=dst, send_sem=send_sem, recv_sem=recv_sem,
                device_id=(dp, peer), device_id_type=MESH,
            ).start()
            return 0

        lax.fori_loop(1, n_space, step, 0)

    cap_sib = sib_copy(capbuf.at[grp, core], capbuf.at[grp, core], 0)
    cap_sib.start()
    wait_bytes(capbuf.at[grp, other], sib_r.at[0])
    grp_send(capbuf.at[grp], cap_s, cap_r)

    @pl.when(jnp.logical_not(first))
    def _():
        wait_bytes(halo.at[0], halo_r.at[0])

    @pl.when(jnp.logical_not(last))
    def _():
        wait_bytes(halo.at[1], halo_r.at[1])

    def fix_tile(ct, _):
        lanes = pl.ds(pl.multiple_of(ct * LANES, LANES), LANES)
        pad = jnp.zeros((HALF - 1, cols, LANES), F32)
        for img in range(images):
            before = halo[0, img, :, :, lanes].astype(F32)
            after = halo[1, img, :, :, lanes].astype(F32)
            xf[img, 0:HALF, :, lanes] = before
            xf[img, HALF + rows : 2 * HALF + rows, :, lanes] = after
            xb = jnp.concatenate([before, pad], axis=0)
            xa = jnp.concatenate([pad, after], axis=0)
            tb = jnp.zeros((HALF, cols, LANES), F32)
            ta = jnp.zeros((HALF, cols, LANES), F32)
            for j in range(TAPS):
                pb = jnp.zeros((HALF, cols, LANES), F32)
                pa = jnp.zeros((HALF, cols, LANES), F32)
                for i in range(HALF):
                    pb = pb + kf[i, j : j + 1, lanes][None] * xb[i : i + HALF]
                    pa = pa + kf[i + HALF + 1, j : j + 1, lanes][None] * xa[i : i + HALF]
                tb = tb + shift_cols(pb, j - HALF)
                ta = ta + shift_cols(pa, j - HALF)
            top = img * tile_pix
            low = top + tile_pix - HALF * cols
            co[top : top + HALF * cols, lanes] += tb.reshape(HALF * cols, LANES)
            co[low : low + HALF * cols, lanes] += ta.reshape(HALF * cols, LANES)
        return 0

    lax.fori_loop(0, ctiles, fix_tile, 0)

    def norm_rows(b, _):
        at = pl.ds(pl.multiple_of(b * ROW_BLOCK, ROW_BLOCK), ROW_BLOCK)
        values = co[at, :]
        center = values - jnp.mean(values, axis=-1, keepdims=True)
        scale = lax.rsqrt(jnp.mean(center * center, axis=-1, keepdims=True) + EPS)
        normed = center * scale
        co[at, :] = normed
        nb[at, :] = normed.astype(BF16)
        inv[at, :] = jnp.broadcast_to(scale, (ROW_BLOCK, LANES))
        return 0

    lax.fori_loop(0, images * tile_pix // ROW_BLOCK, norm_rows, 0)

    load_in.wait()

    def hidden_block(n, _):
        at = pl.ds(pl.multiple_of(n * HID_BLOCK, HID_BLOCK), HID_BLOCK)
        h = dot_nn(nb[...], w_in[:, at])
        square = h * h
        tangent = jnp.tanh(GELU_C * (h + 0.044715 * square * h))
        activated = (0.5 * h * (1.0 + tangent)).astype(BF16).astype(F32)
        for img in range(images):
            asum[img : img + 1, at] = jnp.sum(
                activated[img * tile_pix : (img + 1) * tile_pix], axis=0, keepdims=True
            )
        gp[:, at] = 0.5 * (1.0 + tangent) + 0.5 * h * (1.0 - tangent * tangent) * GELU_C * (
            1.0 + 3.0 * 0.044715 * square
        )
        return 0

    asum[...] = jnp.zeros_like(asum)
    lax.fori_loop(0, hid // HID_BLOCK, hidden_block, 0)

    load_out.wait()
    sums = asum[...]
    high = sums.astype(BF16).astype(F32)
    rest = sums - high
    mid = rest.astype(BF16).astype(F32)
    low = rest - mid
    split = jnp.concatenate([high, mid, low], axis=0).astype(BF16)
    mixed = dot_nn(split, w_out[...])
    mixed = mixed[0:8] + mixed[8:16] + mixed[16:24]
    pool[sp] = mixed[0:images] + ssum[...]
    space_send(lambda peer: pool.at[sp], pool.at[sp], pool_s, pool_r)

    wait_bytes(capbuf.at[pl.ds(0, n_grp - 1)], cap_r)
    for g in range(n_grp):
        for c in range(2):
            r = (2 * g + c) * images
            cap64[r : r + images, :] = capbuf[g, c].astype(F32)
    caps = cap64[...]
    caps_norm = jnp.sqrt(jnp.sum(caps * caps, axis=-1, keepdims=True) + EPS)
    text64[...] = (caps / caps_norm).astype(BF16)

    wait_bytes(pool.at[pl.ds(0, n_space - 1)], pool_r)
    pooled = jnp.sum(pool[...], axis=0) / pixels
    pooled_norm = jnp.sqrt(jnp.sum(pooled * pooled, axis=-1, keepdims=True) + EPS)
    image_unit = pooled / pooled_norm
    image_cast = image_unit.astype(BF16)
    row = lax.broadcasted_iota(jnp.int32, (images, LANES), 0)
    own_pos = jnp.where(row == 0, positives_ref[0], positives_ref[1])
    imgbuf[grp, core, :, 0:chan] = image_cast
    imgbuf[grp, core, :, chan:] = own_pos.astype(F32).astype(BF16)
    img_sib = sib_copy(imgbuf.at[grp, core], imgbuf.at[grp, core], 1)
    img_sib.start()

    text_cast = text64[...]
    logits = LOGIT_SCALE * dot_nt(image_cast, text_cast) + LOGIT_BIAS
    col = lax.broadcasted_iota(jnp.int32, (images, n_img), 1)
    labels = jnp.where(own_pos[:, 0:n_img] == col, 1.0, -1.0)
    pair_grad = (-labels * jax.nn.sigmoid(-labels * logits)).astype(BF16)
    image_side = LOGIT_SCALE * dot_nn(pair_grad, text_cast)
    pooled_grad = (
        image_side - image_unit * jnp.sum(image_unit * image_side, axis=-1, keepdims=True)
    ) / pooled_norm
    slope = (pooled_grad / pixels).astype(BF16)
    agrad[...] = dot_nt(slope, w_out[...])

    def grad_block(n, _):
        at = pl.ds(pl.multiple_of(n * HID_BLOCK, HID_BLOCK), HID_BLOCK)
        for img in range(images):
            pix = slice(img * tile_pix, (img + 1) * tile_pix)
            hg[pix, at] = (agrad[img : img + 1, at] * gp[pix, at]).astype(BF16)
        return 0

    lax.fori_loop(0, hid // HID_BLOCK, grad_block, 0)

    def back_block(c, _):
        at = pl.ds(pl.multiple_of(c * HID_BLOCK, HID_BLOCK), HID_BLOCK)
        cg[:, at] = dot_nt(hg[...], w_in[at, :])
        return 0

    lax.fori_loop(0, chan // HID_BLOCK, back_block, 0)

    wait_bytes(imgbuf.at[grp, other], sib_r.at[1])
    grp_send(imgbuf.at[grp], img_s, img_r)

    def conv_grad_rows(b, _):
        at = pl.ds(pl.multiple_of(b * ROW_BLOCK, ROW_BLOCK), ROW_BLOCK)
        grad = cg[at, :]
        normed = co[at, :]
        m1 = jnp.mean(grad, axis=-1, keepdims=True)
        m2 = jnp.mean(grad * normed, axis=-1, keepdims=True)
        cg[at, :] = inv[at, 0:1] * (grad - m1 - normed * m2)
        return 0

    lax.fori_loop(0, images * tile_pix // ROW_BLOCK, conv_grad_rows, 0)

    def tap_sums(out, tile0):
        def step(t, _):
            lanes = pl.ds(pl.multiple_of((tile0 + t) * LANES, LANES), LANES)
            for j in range(TAPS):
                sums = [jnp.zeros((cols, LANES), F32) for _ in range(TAPS)]
                for img in range(images):
                    grad = cg[img * tile_pix : (img + 1) * tile_pix, lanes]
                    moved = shift_cols(grad.reshape(rows, cols, LANES), HALF - j)
                    for i in range(TAPS):
                        sums[i] = sums[i] + jnp.sum(
                            xf[img, i : i + rows, :, lanes] * moved, axis=0
                        )
                for i in range(TAPS):
                    out[t * (TAPS * TAPS) + i * TAPS + j] = jnp.sum(
                        sums[i], axis=0, keepdims=True
                    )
            return 0

        lax.fori_loop(0, half_tiles, step, 0)

    tap_sums(ksend, half_tiles * other)
    k_sib = sib_copy(ksend.at[pl.ds(0, used)], krecv.at[pl.ds(0, used)], 2)
    k_sib.start()
    kown[pl.ds(used, n_space * chunk - used)] = jnp.zeros((n_space * chunk - used, 1, LANES), F32)
    tap_sums(kown, half_tiles * core)
    wait_bytes(krecv.at[pl.ds(0, used)], sib_r.at[2])
    kown[pl.ds(0, used)] += krecv[pl.ds(0, used)]

    space_send(lambda peer: kown.at[pl.ds(peer * chunk, chunk)], p1.at[sp], p1_s, p1_r)
    p1[sp] = kown[pl.ds(sp * chunk, chunk)]

    wait_bytes(imgbuf.at[pl.ds(0, n_grp - 1)], img_r)
    for g in range(n_grp):
        for c in range(2):
            r = (2 * g + c) * images
            img64[r : r + images, :] = imgbuf[g, c, :, 0:chan].astype(F32)
            pos64[r : r + images, :] = imgbuf[g, c, :, chan:].astype(F32)
    all_img = img64[...].astype(BF16)
    all_logits = LOGIT_SCALE * dot_nt(all_img, text_cast) + LOGIT_BIAS
    all_col = lax.broadcasted_iota(jnp.int32, (n_img, n_img), 1).astype(F32)
    all_labels = jnp.where(pos64[:, 0:n_img] == all_col, 1.0, -1.0)
    score = -all_labels * all_logits
    soft = jnp.maximum(score, 0.0) + jnp.log1p(jnp.exp(-jnp.abs(score)))
    loss_ref[...] = jnp.sum(jnp.sum(soft, axis=1, keepdims=True), axis=0, keepdims=True) / n_img
    all_pair = (-all_labels * jax.nn.sigmoid(score)).astype(BF16)
    own_col = lax.broadcasted_iota(jnp.int32, (images, n_img), 1)
    own_row = lax.broadcasted_iota(jnp.int32, (images, n_img), 0) + dp * images
    pick = jnp.where(own_col == own_row, 1.0, 0.0).astype(BF16)
    own_pair = dot_nt(pick, all_pair).astype(BF16)
    caption_side = LOGIT_SCALE * dot_nn(own_pair, all_img)
    text = captions_ref[...].astype(F32)
    text_norm = jnp.sqrt(jnp.sum(text * text, axis=-1, keepdims=True) + EPS)
    text_unit = text / text_norm
    text_grad_ref[...] = (
        caption_side - text_unit * jnp.sum(text_unit * caption_side, axis=-1, keepdims=True)
    ) / text_norm

    wait_bytes(p1.at[pl.ds(0, n_space - 1)], p1_r)
    p2[grp] = jnp.sum(p1[...], axis=0)
    grp_send(p2.at[grp], p2_s, p2_r)
    wait_bytes(p2.at[pl.ds(0, n_grp - 1)], p2_r)
    mine = kfull.at[core, pl.ds(sp * chunk, chunk)]
    kfull[core, pl.ds(sp * chunk, chunk)] = jnp.sum(p2[...], axis=0)
    space_send(lambda peer: mine, mine, p3_s, p3_r)
    wait_bytes(kfull.at[core, pl.ds(0, (n_space - 1) * chunk)], p3_r)
    full_sib = sib_copy(kfull.at[core, pl.ds(0, used)], kfull.at[core, pl.ds(0, used)], 3)
    full_sib.start()
    wait_bytes(kfull.at[other, pl.ds(0, used)], sib_r.at[3])

    def place(i, _):
        for side in range(2):
            for t in range(half_tiles):
                lane0 = (side * half_tiles + t) * LANES
                for j in range(TAPS):
                    kernel_grad_ref[i, j : j + 1, lane0 : lane0 + LANES] = kfull[
                        side, t * (TAPS * TAPS) + i * TAPS + j
                    ]
        return 0

    lax.fori_loop(0, TAPS, place, 0)

    @pl.when(jnp.logical_not(last))
    def _():
        wait_bytes(halo.at[0], halo_s.at[0])

    @pl.when(jnp.logical_not(first))
    def _():
        wait_bytes(halo.at[1], halo_s.at[1])

    wait_bytes(capbuf.at[grp, core], sib_s.at[0])
    wait_bytes(imgbuf.at[grp, core], sib_s.at[1])
    wait_bytes(ksend.at[pl.ds(0, used)], sib_s.at[2])
    wait_bytes(kfull.at[core, pl.ds(0, used)], sib_s.at[3])
    wait_bytes(capbuf.at[pl.ds(0, n_grp - 1)], cap_s)
    wait_bytes(imgbuf.at[pl.ds(0, n_grp - 1)], img_s)
    wait_bytes(pool.at[pl.ds(0, n_space - 1)], pool_s)
    wait_bytes(p1.at[pl.ds(0, n_space - 1)], p1_s)
    wait_bytes(p2.at[pl.ds(0, n_grp - 1)], p2_s)
    wait_bytes(kfull.at[core, pl.ds(0, (n_space - 1) * chunk)], p3_s)


def solution(mesh):
    n_space, n_dp = mesh.shape["space"], mesh.shape["dp"]
    n_grp = n_dp // 2

    def per_device(scenes, taps, weight_in, weight_out, captions, positives):
        images, rows, cols, chan = scenes.shape
        hid = weight_in.shape[1]
        pix = images * rows * cols
        n_img = images * n_dp
        used = chan // 2 // LANES * TAPS * TAPS
        chunk = -(-used // n_space)
        vmem = pl.BlockSpec(memory_space=pltpu.VMEM)
        hbm = pl.BlockSpec(memory_space=pl.ANY)
        dma = pltpu.SemaphoreType.DMA
        loss, text_grad, kernel_grad = pl.pallas_call(
            functools.partial(kernel, (n_space, n_dp)),
            out_shape=(
                jax.ShapeDtypeStruct((1, 1), F32),
                jax.ShapeDtypeStruct((images, chan), F32),
                jax.ShapeDtypeStruct((TAPS, TAPS, chan), F32),
            ),
            in_specs=[vmem, vmem, hbm, hbm, vmem, pl.BlockSpec(memory_space=pltpu.SMEM)],
            out_specs=(vmem, vmem, vmem),
            scratch_shapes=[
                pltpu.VMEM((images, rows + 2 * HALF, cols, chan), F32),
                pltpu.VMEM((TAPS, TAPS, chan), F32),
                pltpu.VMEM((2, images, HALF, cols, chan), BF16),
                pltpu.VMEM((pix, chan), F32),
                pltpu.VMEM((pix, chan), BF16),
                pltpu.VMEM((pix, LANES), F32),
                pltpu.VMEM((chan, hid), BF16),
                pltpu.VMEM((hid, chan), BF16),
                pltpu.VMEM((pix, hid), F32),
                pltpu.VMEM((8, hid), F32),
                pltpu.VMEM((images, chan), F32),
                pltpu.VMEM((pix, hid), BF16),
                pltpu.VMEM((pix, chan), F32),
                pltpu.VMEM((images, hid), F32),
                pltpu.VMEM((n_space, images, chan), F32),
                pltpu.VMEM((n_grp, 2, images, chan), BF16),
                pltpu.VMEM((n_img, chan), F32),
                pltpu.VMEM((n_img, chan), BF16),
                pltpu.VMEM((n_grp, 2, images, chan + LANES), BF16),
                pltpu.VMEM((n_img, chan), F32),
                pltpu.VMEM((n_img, LANES), F32),
                pltpu.VMEM((n_space * chunk, 1, LANES), F32),
                pltpu.VMEM((n_space * chunk, 1, LANES), F32),
                pltpu.VMEM((n_space * chunk, 1, LANES), F32),
                pltpu.VMEM((n_space, chunk, 1, LANES), F32),
                pltpu.VMEM((n_grp, chunk, 1, LANES), F32),
                pltpu.VMEM((2, n_space * chunk, 1, LANES), F32),
                dma((2,)), dma((2,)), dma((2,)), dma((4,)), dma((4,)),
                dma, dma, dma, dma, dma, dma, dma, dma, dma, dma, dma, dma,
            ],
            compiler_params=pltpu.CompilerParams(
                collective_id=0, has_side_effects=True, vmem_limit_bytes=48 << 20
            ),
        )(scenes, taps, weight_in, weight_out, captions, positives)
        return loss.reshape(()), text_grad, kernel_grad

    return jax.shard_map(
        per_device,
        mesh=mesh,
        in_specs=(P("dp", "space", None, None), P(), P(), P(), P("dp", None), P("dp")),
        out_specs=(P(), P("dp", None), P()),
        check_vma=False,
    )
```

time: 754 us -> 72.7 us (0.10)
  waiting for transfers between devices: 491 us -> 0 us
  blocking collectives: 198 us -> 0 us
  Pallas kernels: 0 us -> 62.2 us
  other arithmetic: 24.8 us -> 0 us
  between operations: 17.7 us -> 2.47 us
  matrix products: 8.13 us -> 0 us
    psum x1 -> x0, waiting for transfers between devices: 268 us -> none  [per_device(): lax.psum((kernel_part, loss_share), ('dp', 'space'))]
    unnamed x3 -> x0, waiting for transfers between devices: 223 us -> none
    psum x2 -> x0, blocking collectives: 140 us -> none  [the longest x1 101 us: per_device(): lax.psum((kernel_part, loss_share), ('dp', 'space'))]
    pallas_call x0 -> x1, Pallas kernels: none -> 62.2 us  [per_device(): pl.pallas_call(functools.partial(kernel, (n_space, n_dp)), out_shape=(jax...]
    all_gather x1 -> x0, blocking collectives: 58.3 us -> none  [per_device(): gathered = lax.all_gather(captions, 'dp', axis=0, tiled=True)]
    reduce_sum x10 -> x0, other arithmetic: 15.6 us -> none  [the longest x1 6.48 us: normalize_rows(): center = conv_out - jnp.mean(conv_out, axis=-1, keepdims=True)]
    dot_general x7 -> x0, matrix products: 8.13 us -> none  [the longest x1 2.52 us: per_device(): act_grad = jnp.dot(slope, weight_out.T, preferred_element_type=jnp.float32)]
  transfers between devices with their start and end apart: 4 -> 0, of which waited for: 2 -> 0; matrix products, arithmetic and copies ran while one was open for 2% -> 0% of each run, Pallas kernels for 0% -> 0%
where the time goes in v1:
time: 72.7 us; the launch traced here: 72.4 us
  Pallas kernels  62.2 us (86%)
  local copies, waits for them, and re-layouts  7.79 us (11%)
  between operations  2.47 us (3%)
    pallas_call x1, Pallas kernels, per_device(): pl.pallas_call(functools.partial(kernel, (n_space, n_dp)), out_shape=(jax...  62.2 us
    unnamed x14, local copies, waits for them, and re-layouts  7.79 us

profile of v1, /device:TPU:1, one launch (start us, length us, event | category | flops | bytes accessed | tf_op | source)
XLA Modules:
  0.0 72.4 jit_solution(1654202553420287206)
XLA Ops:
  0.6 0.0 copy-start
  0.6 1.7 %copy-done = bf16[768,1536]{1,0:T(8,128)(2,1)S(1)} copy-done((bf16[768,1536]{1,0:T(8,128)(2,1)S(1)}, bf16[768,1536]{1,0:T(8,128)(2,1)}, u32[]{:S(2)}) %copy-start) | copy-done | bytes 2359320
  2.3 0.0 copy-start.1
  2.3 1.7 %copy-done.1 = bf16[1536,768]{1,0:T(8,128)(2,1)S(1)} copy-done((bf16[1536,768]{1,0:T(8,128)(2,1)S(1)}, bf16[1536,768]{1,0:T(8,128)(2,1)}, u32[]{:S(2)}) %copy-start.1) | copy-done | bytes 2359320
  4.0 0.0 copy-start.2
  4.0 1.0 %copy-done.2 = bf16[2,14,8,768]{3,2,1,0:T(8,128)(2,1)S(1)} copy-done((bf16[2,14,8,768]{3,2,1,0:T(8,128)(2,1)S(1)}, bf16[2,14,8,768]{3,2,1,0:T(8,128)(2,1)}, u32[]{:S(2)}) %copy-start.2) | copy-done | bytes 344088
  4.9 0.0 copy-start.3
  4.9 0.9 %copy-done.3 = bf16[7,7,768]{2,1,0:T(8,128)(2,1)S(1)} copy-done((bf16[7,7,768]{2,1,0:T(8,128)(2,1)S(1)}, bf16[7,7,768]{2,1,0:T(8,128)(2,1)}, u32[]{:S(2)}) %copy-start.3) | copy-done | bytes 75288
  5.8 0.0 copy-start.4
  5.8 0.7 copy-done.4
  6.5 0.0 copy-start.5
  6.5 0.7 copy-done.5
  7.2 62.2 %shard_map.85 = (f32[1,1]{1,0:T(1,128)}, f32[2,768]{1,0:T(2,128)S(1)}, f32[7,7,768]{2,1,0:T(8,128)S(1)}) custom-call(bf16[2,14,8,768]{3,2,1,0:T(8,128)(2,1)S(1)} %copy-done.2, bf16[7,7,768]{2,1,0:T(8,128)(2,1)S(1)} %copy-done.3, bf16[768,1536]{1,0:T(8,128)(2,1)S(1)} %copy-done, bf16[1536,768]{1,0:T(8,128)(2,1)S(1)} %copy-done.1, ...), custom_call_target="tpu_custom_call" | custom-call | tf_op jit(solution)/shard_map/pallas_call | solution.py:446
  70.0 0.6 copy.13
  70.6 0.7 copy.14
Async XLA Ops:
  0.6 1.7 %copy-start = (bf16[768,1536]{1,0:T(8,128)(2,1)S(1)}, bf16[768,1536]{1,0:T(8,128)(2,1)}, u32[]{:S(2)}) copy-start(bf16[768,1536]{1,0:T(8,128)(2,1)} %w_in_hbm.1) | copy-start | bytes 7077892
  2.3 1.7 %copy-start.1 = (bf16[1536,768]{1,0:T(8,128)(2,1)S(1)}, bf16[1536,768]{1,0:T(8,128)(2,1)}, u32[]{:S(2)}) copy-start(bf16[1536,768]{1,0:T(8,128)(2,1)} %w_out_hbm.1) | copy-start | bytes 7077892
  4.0 1.0 %copy-start.2 = (bf16[2,14,8,768]{3,2,1,0:T(8,128)(2,1)S(1)}, bf16[2,14,8,768]{3,2,1,0:T(8,128)(2,1)}, u32[]{:S(2)}) copy-start(bf16[2,14,8,768]{3,2,1,0:T(8,128)(2,1)} %scenes_ref.1) | copy-start | bytes 1032196
  4.9 0.9 %copy-start.3 = (bf16[7,7,768]{2,1,0:T(8,128)(2,1)S(1)}, bf16[7,7,768]{2,1,0:T(8,128)(2,1)}, u32[]{:S(2)}) copy-start(bf16[7,7,768]{2,1,0:T(8,128)(2,1)} %kernel_ref.1) | copy-start | bytes 225796
  5.8 0.7 copy-start.4
  6.5 0.7 copy-start.5
